TPU v7x, 32 devices: a whole 2x2x4 slice. The times are simulated.
32 devices in a mesh: grp: 2 (over x), wide: 16 (over z, y, core).
Axes of the slice: x: 2, y: 2, z: 4, core: 2. Of those that a mesh axis runs over, the one named last changes fastest.
Arguments:
- raw: bfloat16 [4096, 16, 2048], P(('grp', 'wide')), parts along dimension 0, may hold values from -6 to 6
- cell_feed: int32 [1024], replicated, may hold values from 0 to 1023, each once
- dm_delay: int32 [1024, 1024], replicated, may hold values from 0 to 15
Outputs:
- dedispersed: float32 [2048, 16, 1024], P(('grp', 'wide')), parts along dimension 0
There are 2 independent parts, one for each index of `grp`. A program takes and returns all parts, laid end to end along the dimension named above; an argument that names none is the same for every part. Nothing has to cross between parts.
Inputs may be any that keep to these rules, and one draw needn't show every extreme that they name: `cell_feed`: every antenna stands at exactly one cell.
All inputs are finite; a program needn't handle non-finite values.
Results may differ from a plain program's by a relative error of at most 0.0084.
Values may be sent and summed in bfloat16 or wider, within the bound.
No kernel may reach another device: no remote copies, remote signals or barrier semaphores. Data moves between devices by JAX's collectives and lax.ppermute only.
A program may use at most 128 MiB of HBM per device.

v0:
```python
import math
import jax
import jax.numpy as jnp
import numpy as np
from jax import lax
from jax.sharding import PartitionSpec as P

EAST_COSINE = np.array([[1, 1, 1, 1], [1, 0, -1, 0], [1, -1, 1, -1], [1, 0, -1, 0]], np.float32)
EAST_SINE = np.array([[0, 0, 0, 0], [0, 1, 0, -1], [0, 0, 0, 0], [0, -1, 0, 1]], np.float32)


def phase_pair(count, length):
    angle = (count % length).astype(jnp.float32) * (2.0 * math.pi / length)
    return (jnp.cos(angle), jnp.sin(angle))


def channel_table(samples, width):
    sample_ids = lax.broadcasted_iota(jnp.int32, (samples, width), 0)
    freq_ids = lax.broadcasted_iota(jnp.int32, (samples, width), 1)
    cosine, sine = phase_pair(sample_ids * freq_ids, samples)
    factor = 1.0 / math.sqrt(samples)
    return jnp.concatenate([cosine * factor, -sine * factor], axis=1).astype(jnp.bfloat16)


def sky_table(cells):
    rows = lax.broadcasted_iota(jnp.int32, (cells, cells), 0)
    cols = lax.broadcasted_iota(jnp.int32, (cells, cells), 1)
    cosine, sine = phase_pair(rows * cols, cells)
    real_row = jnp.stack([cosine, sine], axis=-1)
    imag_row = jnp.stack([-sine, cosine], axis=-1)
    factor = 1.0 / math.sqrt(cells)
    return (jnp.stack([real_row, imag_row], axis=1) * factor).astype(jnp.bfloat16)


def transform_table(frames):
    terms = frames // 2 + 1
    harmonic = lax.broadcasted_iota(jnp.int32, (terms, frames), 0)
    moment = lax.broadcasted_iota(jnp.int32, (terms, frames), 1)
    cosine, sine = phase_pair(harmonic * moment, frames)
    return jnp.stack([cosine, -sine]).astype(jnp.bfloat16)


def beam_power(spec, feed_index, table):
    grid = jnp.take(spec, feed_index.reshape(-1), axis=0)
    grid = grid.reshape(feed_index.shape + spec.shape[1:])
    beams = jnp.einsum("joni,penrif->poerfj", table, grid, preferred_element_type=jnp.float32)
    real_part = beams[:, 0]
    imag_part = beams[:, 1]
    cosines = jnp.asarray(EAST_COSINE)
    sines = jnp.asarray(EAST_SINE)
    high = lax.Precision.HIGHEST
    east_real = 0.5 * (
        jnp.einsum("qe,perfj->prfqj", cosines, real_part, precision=high)
        + jnp.einsum("qe,perfj->prfqj", sines, imag_part, precision=high)
    )
    east_imag = 0.5 * (
        jnp.einsum("qe,perfj->prfqj", cosines, imag_part, precision=high)
        - jnp.einsum("qe,perfj->prfqj", sines, real_part, precision=high)
    )
    power = 0.5 * jnp.sum(east_real * east_real + east_imag * east_imag, axis=0)
    return power.reshape(power.shape[0], power.shape[1], -1)


def dedisperse(spectrum, dm_delay, frames):
    base_cos, base_sin = phase_pair(jnp.transpose(dm_delay), frames)
    beams_dev = spectrum.shape[3]
    nfreq = spectrum.shape[2]

    def one_term(carry, block):
        cosine, sine = carry
        cos_half = cosine.astype(jnp.bfloat16)
        sin_half = sine.astype(jnp.bfloat16)
        upper = jnp.concatenate([cos_half, sin_half], axis=1)
        lower = jnp.concatenate([-sin_half, cos_half], axis=1)
        right = jnp.concatenate([upper, lower], axis=0)
        left = block.reshape(2 * nfreq, beams_dev)
        result = lax.dot_general(
            left, right, (((0,), (0,)), ((), ())), preferred_element_type=jnp.float32
        )
        next_cos = cosine * base_cos - sine * base_sin
        next_sin = sine * base_cos + cosine * base_sin
        return ((next_cos, next_sin), result)

    start = (jnp.ones(base_cos.shape, jnp.float32), jnp.zeros(base_cos.shape, jnp.float32))
    final, trials = lax.scan(one_term, start, spectrum)
    return trials.reshape(trials.shape[0], beams_dev, 2, -1)


def synthesis(trials, frames, nfreq):
    terms = frames // 2 + 1
    moment = lax.broadcasted_iota(jnp.int32, (frames, terms), 0)
    harmonic = lax.broadcasted_iota(jnp.int32, (frames, terms), 1)
    cosine, sine = phase_pair(moment * harmonic, frames)
    weight = jnp.where((harmonic == 0) | (harmonic * 2 == frames), 1.0, 2.0).astype(jnp.float32)
    weight = weight / (frames * math.sqrt(nfreq))
    table = jnp.stack([cosine * weight, -sine * weight], axis=1)
    return jnp.einsum("tuk,kbud->btd", table, trials, precision=lax.Precision.HIGHEST)


def body(raw, cell_feed, dm_delay):
    feed_dev, frames, samples = raw.shape
    nfreq = samples // 2
    table = channel_table(samples, nfreq)
    spectra = jnp.dot(
        raw.reshape(feed_dev * frames, samples), table, preferred_element_type=jnp.float32
    )
    spectra = spectra.astype(jnp.bfloat16).reshape(feed_dev, frames, 2, nfreq)
    cells = cell_feed.shape[0] // 4
    polar = lax.broadcasted_iota(jnp.int32, (2, 4, cells), 0)
    feed_index = 2 * cell_feed.reshape(1, 4, cells) + polar
    table_sky = sky_table(cells)
    arrived = lax.all_to_all(spectra, "wide", split_axis=3, concat_axis=0, tiled=True)
    power = beam_power(arrived, feed_index, table_sky)
    centred = (power - jnp.mean(power, axis=0, keepdims=True)).astype(jnp.bfloat16)
    time_table = transform_table(frames)
    local = jnp.einsum("okr,rfb->kofb", time_table, centred, preferred_element_type=jnp.float32)
    spectrum = lax.all_to_all(
        local.astype(jnp.bfloat16), "wide", split_axis=3, concat_axis=2, tiled=True
    )
    trials = dedisperse(spectrum, dm_delay, frames)
    return synthesis(trials, frames, nfreq)


def solution(mesh):
    placed = (P(("grp", "wide"), None, None), P(), P())
    return jax.shard_map(
        body, mesh=mesh, in_specs=placed, out_specs=P(("grp", "wide"), None, None), check_vma=False
    )
```

profile of v0, /device:TPU:13, one launch (start us, length us, event | category | flops | bytes accessed | tf_op | source)
XLA Modules:
  0.0 774.5 jit_solution(11408778004443474924)
XLA Ops:
  0.0 34.1 %multiply_convert_fusion = (bf16[2048,1024]{1,0:T(8,128)(2,1)S(1)}, bf16[2048,1024]{1,0:T(8,128)(2,1)S(1)}) fusion(), kind=kLoop, calls=%fused_computation.36 | loop fusion | flops 39845888 | bytes 8388608 | tf_op jit(solution)/shard_map/convert.3
  34.1 20.6 %convert_bitcast_fusion = bf16[2048,2048]{0,1:T(8,128)(2,1)} fusion(bf16[2048,2048]{1,0:T(8,128)(2,1)S(1)} %bitcast.101, bf16[2048,1024]{1,0:T(8,128)(2,1)S(1)} %get-tuple-element.115, bf16[2048,1024]{1,0:T(8,128)(2,1)S(1)} %get-tuple-element.116), kind=kOutput, calls=%fused_computation.35 | convolution fusion | flops 17200840704 | bytes 25165824 | tf_op jit(solution)/shard_map/dot_general | solution.py:104
  54.7 12.4 %copy.57 = bf16[2048,2048]{1,0:T(8,128)(2,1)} copy(bf16[2048,2048]{0,1:T(8,128)(2,1)} %convert_bitcast_fusion) | data formatting | bytes 16777216 | tf_op jit(solution)/shard_map/convert_element_type | solution.py:107
  67.1 14.5 %reshape.314 = bf16[128,16,2,1024]{3,2,1,0:T(2,128)(2,1)} reshape(bf16[2048,2048]{1,0:T(8,128)(2,1)} %copy.57) | data formatting | bytes 16777216 | tf_op jit(solution)/shard_map/reshape | solution.py:107
  81.6 16.8 %copy.58 = bf16[128,16,2,1024]{0,1,2,3:T(8,128)(2,1)} copy(bf16[128,16,2,1024]{3,2,1,0:T(2,128)(2,1)} %reshape.314) | data formatting | bytes 16777216 | tf_op jit(solution)/shard_map/reshape | solution.py:107
  98.4 7.0 all-to-all-start
  107.7 179.9 %all-to-all-done = bf16[128,16,2,1024]{0,1,2,3:T(8,128)(2,1)} async-done(((bf16[128,16,2,1024]{0,1,2,3:T(8,128)(2,1)}), bf16[128,16,2,1024]{0,1,2,3:T(8,128)(2,1)}, u32[]{:S(2)}, u32[]{:S(2)}) %all-to-all-start) | async-done | bytes 8388640 | tf_op jit(solution)/shard_map/all_to_all | solution.py:112
  287.6 29.0 %copy.82 = bf16[16,128,16,2,64]{4,2,3,1,0:T(8,128)(2,1)} copy(bf16[16,128,16,2,64]{1,2,3,4,0:T(8,128)(2,1)} %bitcast.5) | data formatting | bytes 16777216 | tf_op jit(solution)/shard_map/all_to_all | solution.py:112
  316.7 25.0 %gather_fusion = bf16[2048,16,2,64]{3,1,2,0:T(8,128)(2,1)} fusion(bf16[2048,16,2,64]{3,1,2,0:T(8,128)(2,1)} %bitcast.92, s32[2048]{0:T(1024)S(1)} %broadcast_clamp_fusion), kind=kCustom, calls=%fused_computation | custom fusion | bytes 16785408 | tf_op jit(solution)/shard_map/jit(_take)/gather | solution.py:44
  341.7 19.8 %copy.83 = bf16[2,4,256,16,2,64]{2,1,0,5,4,3:T(4,128)(2,1)} copy(bf16[2,4,256,16,2,64]{5,3,4,2,1,0:T(8,128)(2,1)} %bitcast.93) | data formatting | bytes 16777216 | tf_op jit(solution)/shard_map/jit(_take)/gather | solution.py:44
  361.4 5.8 select_bitcast_fusion
  367.2 8.2 %fusion.39 = f32[2,2,4,16,64,256]{5,4,1,3,2,0:T(8,128)} fusion(bf16[2,4,256,16,2,64,1]{2,1,0,5,4,3,6:T(4,128)(2,1)S(1)} %select_bitcast_fusion, f32[256,1,256,2]{2,0,3,1:T(8,128)S(1)} %get-tuple-element.112, f32[256,1,256,2]{2,0,3,1:T(8,128)S(1)} %get-tuple-element.111), kind=kOutput, calls=%fused_computation.49 | convolution fusion | flops 4295753728 | bytes 26214400 | tf_op jit(solution)/shard_map/joni,penrif->poerfj/dot_general | solution.py:46
  375.4 6.5 slice_bitcast_fusion.1
  382.0 18.8 %fusion.31 = f32[2,16,64,256,4]{3,4,2,1,0:T(4,128)} fusion(f32[4,4,1,1,1]{1,0,4,3,2:T(4,128)S(1)} %copy-done.3, f32[2,4,16,64,256]{4,3,2,1,0:T(8,128)S(1)} %get-tuple-element.108), kind=kOutput, calls=%fused_computation.41 | convolution fusion | flops 100663296 | bytes 16777280 | tf_op jit(solution)/shard_map/qe,perfj->prfqj/dot_general | solution.py:57
  400.8 18.4 %fusion.33 = f32[2,16,64,256,4]{3,4,2,1,0:T(4,128)} fusion(f32[4,4,1,1,1]{1,0,4,3,2:T(4,128)S(1)} %copy-done.4, f32[2,4,16,64,256]{4,3,2,1,0:T(8,128)S(1)} %get-tuple-element.108), kind=kOutput, calls=%fused_computation.43 | convolution fusion | flops 100663296 | bytes 16777280 | tf_op jit(solution)/shard_map/qe,perfj->prfqj/dot_general | solution.py:54
  419.2 18.5 %fusion.35 = f32[2,16,64,256,4]{3,4,2,1,0:T(4,128)} fusion(f32[4,4,1,1,1]{1,0,4,3,2:T(4,128)S(1)} %copy-done.4, f32[2,4,16,64,256]{4,3,2,1,0:T(8,128)S(1)} %get-tuple-element.107), kind=kOutput, calls=%fused_computation.45 | convolution fusion | flops 100663296 | bytes 16777280 | tf_op jit(solution)/shard_map/qe,perfj->prfqj/dot_general | solution.py:58
  437.7 32.8 %add_reduce_fusion = f32[16,64,256,4]{2,3,1,0:T(4,128)} fusion(f32[2,16,64,256,4]{3,4,2,1,0:T(4,128)} %fusion.31, f32[2,16,64,256,4]{3,4,2,1,0:T(4,128)} %fusion.35, f32[2,16,64,256,4]{3,4,2,1,0:T(4,128)} %fusion.33, f32[4,4,1,1,1]{1,0,4,3,2:T(4,128)S(1)} %copy-done.3, f32[2,4,16,64,256]{4,3,2,1,0:T(8,128)} %copy-done.1), kind=kOutput, calls=%fused_computation.33 | convolution fusion | flops 116391936 | bytes 37748800 | tf_op jit(solution)/shard_map/qe,perfj->prfqj/dot_general | solution.py:53
  470.5 5.4 multiply_bitcast_fusion
  476.9 5.8 mul.255
  482.8 7.1 convert_bitcast_fusion.1
  489.9 14.7 %copy.69 = bf16[9,2,64,1024]{2,1,0,3:T(2,128)(2,1)} copy(bf16[9,2,64,1024]{3,0,1,2:T(8,128)(2,1)} %convert_bitcast_fusion.1) | data formatting | bytes 4718592 | tf_op jit(solution)/shard_map/convert_element_type | solution.py:118
  504.6 7.8 %reshape.334 = bf16[16,2,36864]{2,1,0:T(2,128)(2,1)} reshape(bf16[1024,9,2,64]{3,2,1,0:T(2,128)(2,1)} %bitcast.94) | data formatting | bytes 4718592
  512.5 5.1 all-to-all-start.1
  517.6 5.3 copy.56
  523.0 18.4 %fusion.55 = (f32[1024,1024]{1,0:T(8,128)}, f32[1024,1024]{1,0:T(8,128)}) fusion(s32[1024,1024]{0,1:T(8,128)} %copy.56), kind=kLoop, calls=%fused_computation.65 | loop fusion | flops 13631488 | bytes 12582912 | tf_op jit(solution)/shard_map/sin | solution.py:14
  541.4 29.1 %all-to-all-done.1 = bf16[16,2,36864]{2,1,0:T(2,128)(2,1)S(1)} async-done(((bf16[16,2,36864]{2,1,0:T(2,128)(2,1)}), bf16[16,2,36864]{2,1,0:T(2,128)(2,1)S(1)}, u32[]{:S(2)}, u32[]{:S(2)}) %all-to-all-start.1) | async-done | bytes 2359328 | tf_op jit(solution)/shard_map/all_to_all | solution.py:117
  570.5 5.3 reshape.335
  575.8 11.5 %copy.90 = bf16[9,2,64,16,64]{4,2,3,1,0:T(8,128)(2,1)} copy(bf16[9,2,64,16,64]{2,1,0,4,3:T(2,128)(2,1)} %bitcast.95) | data formatting | bytes 4718592 | tf_op jit(solution)/shard_map/all_to_all | solution.py:117
  587.2 166.2 %while.15 = (s32[]{:T(128)}, f32[1024,1024]{1,0:T(8,128)}, f32[1024,1024]{1,0:T(8,128)}, f32[9,64,2048]{2,1,0:T(8,128)}, f32[1024,1024]{1,0:T(8,128)}, /*index=5...) while((s32[]{:T(128)}, f32[1024,1024]{1,0:T(8,128)}, ...), condition=%wide.region_3.4_spmd.clone, body=%wide.region_2.3_spmd.clone.sunk | while | flops 584056832 | bytes 64225924 | solution.py:85
  592.3 8.2 %multiply_add_fusion.2 = (f32[1024,1024]{1,0:T(8,128)}, f32[1024,1024]{1,0:T(8,128)}) fusion(f32[1024,1024]{1,0:T(8,128)S(1)} %copy-done, f32[1024,1024]{1,0:T(8,128)} %get-tuple-element.196, f32[1024,1024]{1,0:T(8,128)} %get-tuple-element.185, f32[1024,1024]{1,0:T(8,128)} %get-tuple-element.184, pred[]{:T(512)S(6)} %compare.38), kind=kLoop, calls=%fused_computation.9.clone.1 | loop fusion | flops 8388608 | bytes 25165824 | tf_op jit(solution)/shard_map/while/body/eval_jaxpr/add | solution.py:81
  600.4 4.9 fusion.105
  608.9 10.6 %multiply_add_fusion.2 = (f32[1024,1024]{1,0:T(8,128)}, f32[1024,1024]{1,0:T(8,128)}) fusion(f32[1024,1024]{1,0:T(8,128)S(1)} %copy-done, f32[1024,1024]{1,0:T(8,128)} %get-tuple-element.196, f32[1024,1024]{1,0:T(8,128)} %get-tuple-element.185, f32[1024,1024]{1,0:T(8,128)} %get-tuple-element.184, pred[]{:T(512)S(6)} %compare.38), kind=kLoop, calls=%fused_computation.9.clone.1 | loop fusion | flops 8388608 | bytes 25165824 | tf_op jit(solution)/shard_map/while/body/eval_jaxpr/add | solution.py:81
  619.6 4.9 fusion.105
  628.1 10.6 %multiply_add_fusion.2 = (f32[1024,1024]{1,0:T(8,128)}, f32[1024,1024]{1,0:T(8,128)}) fusion(f32[1024,1024]{1,0:T(8,128)S(1)} %copy-done, f32[1024,1024]{1,0:T(8,128)} %get-tuple-element.196, f32[1024,1024]{1,0:T(8,128)} %get-tuple-element.185, f32[1024,1024]{1,0:T(8,128)} %get-tuple-element.184, pred[]{:T(512)S(6)} %compare.38), kind=kLoop, calls=%fused_computation.9.clone.1 | loop fusion | flops 8388608 | bytes 25165824 | tf_op jit(solution)/shard_map/while/body/eval_jaxpr/add | solution.py:81
  638.7 4.9 fusion.105
  647.2 10.6 %multiply_add_fusion.2 = (f32[1024,1024]{1,0:T(8,128)}, f32[1024,1024]{1,0:T(8,128)}) fusion(f32[1024,1024]{1,0:T(8,128)S(1)} %copy-done, f32[1024,1024]{1,0:T(8,128)} %get-tuple-element.196, f32[1024,1024]{1,0:T(8,128)} %get-tuple-element.185, f32[1024,1024]{1,0:T(8,128)} %get-tuple-element.184, pred[]{:T(512)S(6)} %compare.38), kind=kLoop, calls=%fused_computation.9.clone.1 | loop fusion | flops 8388608 | bytes 25165824 | tf_op jit(solution)/shard_map/while/body/eval_jaxpr/add | solution.py:81
  657.8 4.9 fusion.105
  666.3 10.6 %multiply_add_fusion.2 = (f32[1024,1024]{1,0:T(8,128)}, f32[1024,1024]{1,0:T(8,128)}) fusion(f32[1024,1024]{1,0:T(8,128)S(1)} %copy-done, f32[1024,1024]{1,0:T(8,128)} %get-tuple-element.196, f32[1024,1024]{1,0:T(8,128)} %get-tuple-element.185, f32[1024,1024]{1,0:T(8,128)} %get-tuple-element.184, pred[]{:T(512)S(6)} %compare.38), kind=kLoop, calls=%fused_computation.9.clone.1 | loop fusion | flops 8388608 | bytes 25165824 | tf_op jit(solution)/shard_map/while/body/eval_jaxpr/add | solution.py:81
  676.9 4.9 fusion.105
  685.4 10.6 %multiply_add_fusion.2 = (f32[1024,1024]{1,0:T(8,128)}, f32[1024,1024]{1,0:T(8,128)}) fusion(f32[1024,1024]{1,0:T(8,128)S(1)} %copy-done, f32[1024,1024]{1,0:T(8,128)} %get-tuple-element.196, f32[1024,1024]{1,0:T(8,128)} %get-tuple-element.185, f32[1024,1024]{1,0:T(8,128)} %get-tuple-element.184, pred[]{:T(512)S(6)} %compare.38), kind=kLoop, calls=%fused_computation.9.clone.1 | loop fusion | flops 8388608 | bytes 25165824 | tf_op jit(solution)/shard_map/while/body/eval_jaxpr/add | solution.py:81
  696.0 4.9 fusion.105
  704.5 10.6 %multiply_add_fusion.2 = (f32[1024,1024]{1,0:T(8,128)}, f32[1024,1024]{1,0:T(8,128)}) fusion(f32[1024,1024]{1,0:T(8,128)S(1)} %copy-done, f32[1024,1024]{1,0:T(8,128)} %get-tuple-element.196, f32[1024,1024]{1,0:T(8,128)} %get-tuple-element.185, f32[1024,1024]{1,0:T(8,128)} %get-tuple-element.184, pred[]{:T(512)S(6)} %compare.38), kind=kLoop, calls=%fused_computation.9.clone.1 | loop fusion | flops 8388608 | bytes 25165824 | tf_op jit(solution)/shard_map/while/body/eval_jaxpr/add | solution.py:81
  715.2 4.9 fusion.105
  723.7 10.6 %multiply_add_fusion.2 = (f32[1024,1024]{1,0:T(8,128)}, f32[1024,1024]{1,0:T(8,128)}) fusion(f32[1024,1024]{1,0:T(8,128)S(1)} %copy-done, f32[1024,1024]{1,0:T(8,128)} %get-tuple-element.196, f32[1024,1024]{1,0:T(8,128)} %get-tuple-element.185, f32[1024,1024]{1,0:T(8,128)} %get-tuple-element.184, pred[]{:T(512)S(6)} %compare.38), kind=kLoop, calls=%fused_computation.9.clone.1 | loop fusion | flops 8388608 | bytes 25165824 | tf_op jit(solution)/shard_map/while/body/eval_jaxpr/add | solution.py:81
  734.3 4.9 fusion.105
  742.8 10.6 %multiply_add_fusion.2 = (f32[1024,1024]{1,0:T(8,128)}, f32[1024,1024]{1,0:T(8,128)}) fusion(f32[1024,1024]{1,0:T(8,128)S(1)} %copy-done, f32[1024,1024]{1,0:T(8,128)} %get-tuple-element.196, f32[1024,1024]{1,0:T(8,128)} %get-tuple-element.185, f32[1024,1024]{1,0:T(8,128)} %get-tuple-element.184, pred[]{:T(512)S(6)} %compare.38), kind=kLoop, calls=%fused_computation.9.clone.1 | loop fusion | flops 8388608 | bytes 25165824 | tf_op jit(solution)/shard_map/while/body/eval_jaxpr/add | solution.py:81
  753.5 7.4 reshape.315
  760.8 13.1 %fusion.48 = f32[64,16,1024]{2,1,0:T(8,128)} fusion(f32[9,64,2,1024]{3,2,1,0:T(2,128)} %reshape.315, f32[16,1,9]{2,0,1:T(8,128)S(1)} %get-tuple-element.114, f32[16,1,9]{2,0,1:T(8,128)S(1)} %get-tuple-element.113), kind=kOutput, calls=%fused_computation.60 | convolution fusion | flops 226492704 | bytes 8914048 | tf_op jit(solution)/shard_map/tuk,kbud->btd/dot_general | solution.py:97
  (68 shorter events, 36.6 us)
Async XLA Ops:
  0.0 34.1 %copy-start.6 = (bf16[128,16,2048]{2,1,0:T(8,128)(2,1)S(1)}, bf16[128,16,2048]{2,1,0:T(8,128)(2,1)}, u32[]{:S(2)}) copy-start(bf16[128,16,2048]{2,1,0:T(8,128)(2,1)} %param.7) | copy-start | bytes 25165828
  98.4 7.0 copy-start.5
  98.4 189.2 %all-to-all-start = ((bf16[128,16,2,1024]{0,1,2,3:T(8,128)(2,1)}), bf16[128,16,2,1024]{0,1,2,3:T(8,128)(2,1)}, u32[]{:S(2)}, u32[]{:S(2)}) async-start(bf16[128,16,2,1024]{0,1,2,3:T(8,128)(2,1)} %copy.58), calls=%async_computation | async-start | bytes 16777216 | tf_op jit(solution)/shard_map/all_to_all | solution.py:112
  375.4 6.5 copy-start.3
  381.9 37.2 %copy-start.1 = (f32[2,4,16,64,256]{4,3,2,1,0:T(8,128)}, f32[2,4,16,64,256]{4,3,2,1,0:T(8,128)S(1)}, u32[]{:S(2)}) copy-start(f32[2,4,16,64,256]{4,3,2,1,0:T(8,128)S(1)} %get-tuple-element.107) | copy-start | bytes 25165828
  382.0 18.8 %copy-start.4 = (f32[4,4,1,1,1]{1,0,4,3,2:T(4,128)S(1)}, f32[4,4,1,1,1]{1,0,4,3,2:T(4,128)}, u32[]{:S(2)}) copy-start(f32[4,4,1,1,1]{1,0,4,3,2:T(4,128)} %constant.123) | copy-start | bytes 196
  470.5 5.4 copy-start.2
  512.5 58.0 %all-to-all-start.1 = ((bf16[16,2,36864]{2,1,0:T(2,128)(2,1)}), bf16[16,2,36864]{2,1,0:T(2,128)(2,1)S(1)}, u32[]{:S(2)}, u32[]{:S(2)}) async-start(bf16[16,2,36864]{2,1,0:T(2,128)(2,1)} %reshape.334), calls=%async_computation.1 | async-start | bytes 4718592 | tf_op jit(solution)/shard_map/all_to_all | solution.py:117
  589.8 2.4 copy-start
  606.5 2.5 copy-start
  625.6 2.4 copy-start
  644.7 2.4 copy-start
  663.8 2.4 copy-start
  682.9 2.4 copy-start
  702.1 2.5 copy-start
  721.2 2.5 copy-start
  740.4 2.5 copy-start
where the time goes:
time: 784 us; the launch traced here: 774 us
  waiting for transfers between devices  209 us (27%)
  other arithmetic  201 us (26%)
  local copies, waits for them, and re-layouts  192 us (24%)
  matrix products  160 us (20%)
  starting transfers between devices  12.1 us (2%)
    all_to_all x1, waiting for transfers between devices, body(): lax.all_to_all(spectra, 'wide', split_axis=3, concat_axis=0, tiled=True)  180 us
    add x9, other arithmetic, one_term(): next_sin = sine * base_cos + cosine * base_sin  93.3 us
    gather x2, local copies, waits for them, and re-layouts, beam_power(): grid = jnp.take(spec, feed_index.reshape(-1), axis=0)  44.8 us
    neg x9, other arithmetic, one_term(): lower = jnp.concatenate([-sin_half, cos_half], axis=1)  41 us
    another operation x2, other arithmetic  34.1 us
    dot_general x1, matrix products, beam_power(): jnp.einsum('qe,perfj->prfqj', cosines, real_part, precision=high)  32.8 us
    reshape x2, local copies, waits for them, and re-layouts, body(): spectra = spectra.astype(jnp.bfloat16).reshape(feed_dev, frames, 2, nfreq)  31.3 us
    all_to_all x1, waiting for transfers between devices, body(): lax.all_to_all(local.astype(jnp.bfloat16), 'wide', split_axis=3, concat_a...  29.1 us
  transfers between devices with their start and end apart: 2, of which 2 were waited for; matrix products, arithmetic and copies ran while one was open for 3% of the time, Pallas kernels for 0%

commit v1 on v0

--- a/solution.py
+++ b/solution.py
@@ -114,8 +114,14 @@
     centred = (power - jnp.mean(power, axis=0, keepdims=True)).astype(jnp.bfloat16)
     time_table = transform_table(frames)
     local = jnp.einsum("okr,rfb->kofb", time_table, centred, preferred_element_type=jnp.float32)
-    spectrum = lax.all_to_all(
-        local.astype(jnp.bfloat16), "wide", split_axis=3, concat_axis=2, tiled=True
+    spectrum = jnp.concatenate(
+        lax.all_to_all(
+            jnp.stack(jnp.split(local.astype(jnp.bfloat16), lax.axis_size("wide"), axis=3)),
+            "wide",
+            0,
+            0,
+        ),
+        axis=2,
     )
     trials = dedisperse(spectrum, dm_delay, frames)
     return synthesis(trials, frames, nfreq)

time: 784 us -> 770 us (0.982)
  local copies, waits for them, and re-layouts: 192 us -> 180 us
    convert_element_type x1 -> x0, local copies, waits for them, and re-layouts: 14.7 us -> none  [body(): local.astype(jnp.bfloat16)]
    all_to_all x1 -> x0, local copies, waits for them, and re-layouts: 11.5 us -> none  [body(): lax.all_to_all(local.astype(jnp.bfloat16), 'wide', split_axis=3, concat_a...]
    unnamed x16 -> x32, local copies, waits for them, and re-layouts: 18.5 us -> 28.2 us
where the time goes in v1:
time: 770 us; the launch traced here: 761 us
  waiting for transfers between devices  209 us (27%)
  other arithmetic  201 us (26%)
  local copies, waits for them, and re-layouts  180 us (23%)
  matrix products  158 us (21%)
  starting transfers between devices  12.3 us (2%)
    all_to_all x1, waiting for transfers between devices, body(): lax.all_to_all(spectra, 'wide', split_axis=3, concat_axis=0, tiled=True)  180 us
    add x9, other arithmetic, one_term(): next_sin = sine * base_cos + cosine * base_sin  93.3 us
    gather x2, local copies, waits for them, and re-layouts, beam_power(): grid = jnp.take(spec, feed_index.reshape(-1), axis=0)  44.8 us
    neg x9, other arithmetic, one_term(): lower = jnp.concatenate([-sin_half, cos_half], axis=1)  41 us
    another operation x2, other arithmetic  34.1 us
    dot_general x1, matrix products, beam_power(): jnp.einsum('qe,perfj->prfqj', cosines, real_part, precision=high)  32.8 us
    reshape x2, local copies, waits for them, and re-layouts, body(): spectra = spectra.astype(jnp.bfloat16).reshape(feed_dev, frames, 2, nfreq)  31.3 us
    all_to_all x1, waiting for transfers between devices, body(): lax.all_to_all(jnp.stack(jnp.split(local.astype(jnp.bfloat16), lax.axis_s...  29.1 us
  transfers between devices with their start and end apart: 2, of which 2 were waited for; matrix products, arithmetic and copies ran while one was open for 3% of the time, Pallas kernels for 0%

profile of v1, /device:TPU:13, one launch (start us, length us, event | category | flops | bytes accessed | tf_op | source)
XLA Modules:
  0.0 760.5 jit_solution(18321137730962282944)
XLA Ops:
  0.0 34.1 %multiply_convert_fusion = (bf16[2048,1024]{1,0:T(8,128)(2,1)S(1)}, bf16[2048,1024]{1,0:T(8,128)(2,1)S(1)}) fusion(), kind=kLoop, calls=%fused_computation.36 | loop fusion | flops 39845888 | bytes 8388608 | tf_op jit(solution)/shard_map/convert.3
  34.1 20.6 %convert_bitcast_fusion = bf16[2048,2048]{0,1:T(8,128)(2,1)} fusion(bf16[2048,2048]{1,0:T(8,128)(2,1)S(1)} %bitcast.158, bf16[2048,1024]{1,0:T(8,128)(2,1)S(1)} %get-tuple-element.129, bf16[2048,1024]{1,0:T(8,128)(2,1)S(1)} %get-tuple-element.130), kind=kOutput, calls=%fused_computation.35 | convolution fusion | flops 17200840704 | bytes 25165824 | tf_op jit(solution)/shard_map/dot_general | solution.py:104
  54.7 12.4 %copy.69 = bf16[2048,2048]{1,0:T(8,128)(2,1)} copy(bf16[2048,2048]{0,1:T(8,128)(2,1)} %convert_bitcast_fusion) | data formatting | bytes 16777216 | tf_op jit(solution)/shard_map/convert_element_type | solution.py:107
  67.1 14.5 %reshape.320 = bf16[128,16,2,1024]{3,2,1,0:T(2,128)(2,1)} reshape(bf16[2048,2048]{1,0:T(8,128)(2,1)} %copy.69) | data formatting | bytes 16777216 | tf_op jit(solution)/shard_map/reshape | solution.py:107
  81.6 16.8 %copy.70 = bf16[128,16,2,1024]{0,1,2,3:T(8,128)(2,1)} copy(bf16[128,16,2,1024]{3,2,1,0:T(2,128)(2,1)} %reshape.320) | data formatting | bytes 16777216 | tf_op jit(solution)/shard_map/reshape | solution.py:107
  98.4 7.1 all-to-all-start
  107.8 179.9 %all-to-all-done = bf16[128,16,2,1024]{0,1,2,3:T(8,128)(2,1)} async-done(((bf16[128,16,2,1024]{0,1,2,3:T(8,128)(2,1)}), bf16[128,16,2,1024]{0,1,2,3:T(8,128)(2,1)}, u32[]{:S(2)}, u32[]{:S(2)}) %all-to-all-start) | async-done | bytes 8388640 | tf_op jit(solution)/shard_map/all_to_all | solution.py:112
  287.7 29.0 %copy.93 = bf16[16,128,16,2,64]{4,2,3,1,0:T(8,128)(2,1)} copy(bf16[16,128,16,2,64]{1,2,3,4,0:T(8,128)(2,1)} %bitcast.5) | data formatting | bytes 16777216 | tf_op jit(solution)/shard_map/all_to_all | solution.py:112
  316.7 25.0 %gather_fusion = bf16[2048,16,2,64]{3,1,2,0:T(8,128)(2,1)} fusion(bf16[2048,16,2,64]{3,1,2,0:T(8,128)(2,1)} %bitcast.150, s32[2048]{0:T(1024)S(1)} %broadcast_clamp_fusion), kind=kCustom, calls=%fused_computation | custom fusion | bytes 16785408 | tf_op jit(solution)/shard_map/jit(_take)/gather | solution.py:44
  341.7 19.8 %copy.94 = bf16[2,4,256,16,2,64]{2,1,0,5,4,3:T(4,128)(2,1)} copy(bf16[2,4,256,16,2,64]{5,3,4,2,1,0:T(8,128)(2,1)} %bitcast.151) | data formatting | bytes 16777216 | tf_op jit(solution)/shard_map/jit(_take)/gather | solution.py:44
  361.5 5.8 select_bitcast_fusion
  367.3 8.2 %fusion.39 = f32[2,2,4,16,64,256]{5,4,1,3,2,0:T(8,128)} fusion(bf16[2,4,256,16,2,64,1]{2,1,0,5,4,3,6:T(4,128)(2,1)S(1)} %select_bitcast_fusion, f32[256,1,256,2]{2,0,3,1:T(8,128)S(1)} %get-tuple-element.126, f32[256,1,256,2]{2,0,3,1:T(8,128)S(1)} %get-tuple-element.125), kind=kOutput, calls=%fused_computation.49 | convolution fusion | flops 4295753728 | bytes 26214400 | tf_op jit(solution)/shard_map/joni,penrif->poerfj/dot_general | solution.py:46
  375.5 6.5 slice_bitcast_fusion.1
  382.1 18.9 %fusion.31 = f32[2,16,64,256,4]{3,4,2,1,0:T(4,128)} fusion(f32[4,4,1,1,1]{1,0,4,3,2:T(4,128)S(1)} %copy-done.3, f32[2,4,16,64,256]{4,3,2,1,0:T(8,128)S(1)} %get-tuple-element.122), kind=kOutput, calls=%fused_computation.41 | convolution fusion | flops 100663296 | bytes 16777280 | tf_op jit(solution)/shard_map/qe,perfj->prfqj/dot_general | solution.py:57
  401.0 18.4 %fusion.33 = f32[2,16,64,256,4]{3,4,2,1,0:T(4,128)} fusion(f32[4,4,1,1,1]{1,0,4,3,2:T(4,128)S(1)} %copy-done.4, f32[2,4,16,64,256]{4,3,2,1,0:T(8,128)S(1)} %get-tuple-element.122), kind=kOutput, calls=%fused_computation.43 | convolution fusion | flops 100663296 | bytes 16777280 | tf_op jit(solution)/shard_map/qe,perfj->prfqj/dot_general | solution.py:54
  419.4 18.5 %fusion.35 = f32[2,16,64,256,4]{3,4,2,1,0:T(4,128)} fusion(f32[4,4,1,1,1]{1,0,4,3,2:T(4,128)S(1)} %copy-done.4, f32[2,4,16,64,256]{4,3,2,1,0:T(8,128)S(1)} %get-tuple-element.121), kind=kOutput, calls=%fused_computation.45 | convolution fusion | flops 100663296 | bytes 16777280 | tf_op jit(solution)/shard_map/qe,perfj->prfqj/dot_general | solution.py:58
  437.9 32.8 %add_reduce_fusion = f32[16,64,256,4]{2,3,1,0:T(4,128)} fusion(f32[2,16,64,256,4]{3,4,2,1,0:T(4,128)} %fusion.31, f32[2,16,64,256,4]{3,4,2,1,0:T(4,128)} %fusion.35, f32[2,16,64,256,4]{3,4,2,1,0:T(4,128)} %fusion.33, f32[4,4,1,1,1]{1,0,4,3,2:T(4,128)S(1)} %copy-done.3, f32[2,4,16,64,256]{4,3,2,1,0:T(8,128)} %copy-done.1), kind=kOutput, calls=%fused_computation.33 | convolution fusion | flops 116391936 | bytes 37748800 | tf_op jit(solution)/shard_map/qe,perfj->prfqj/dot_general | solution.py:53
  470.7 5.4 multiply_bitcast_fusion
  477.1 5.8 mul.255
  483.0 5.1 convert_bitcast_fusion.1
  492.2 4.2 copy.81
  496.4 7.8 %reshape.342 = bf16[16,2,36864]{2,1,0:T(2,128)(2,1)} reshape(bf16[16,9,2,64,64]{4,3,2,1,0:T(8,128)(2,1)} %copy.81) | data formatting | bytes 4718592
  504.2 5.2 all-to-all-start.1
  509.5 5.3 copy.68
  514.9 18.4 %fusion.55 = (f32[1024,1024]{1,0:T(8,128)}, f32[1024,1024]{1,0:T(8,128)}) fusion(s32[1024,1024]{0,1:T(8,128)} %copy.68), kind=kLoop, calls=%fused_computation.65 | loop fusion | flops 13631488 | bytes 12582912 | tf_op jit(solution)/shard_map/sin | solution.py:14
  533.3 29.1 %all-to-all-done.1 = bf16[16,2,36864]{2,1,0:T(2,128)(2,1)S(1)} async-done(((bf16[16,2,36864]{2,1,0:T(2,128)(2,1)}), bf16[16,2,36864]{2,1,0:T(2,128)(2,1)S(1)}, u32[]{:S(2)}, u32[]{:S(2)}) %all-to-all-start.1) | async-done | bytes 2359328 | tf_op jit(solution)/shard_map/all_to_all | solution.py:118
  562.4 5.3 reshape.343
  567.7 6.0 copy.97
  573.7 166.2 %while.15 = (s32[]{:T(128)}, f32[1024,1024]{1,0:T(8,128)}, f32[1024,1024]{1,0:T(8,128)}, f32[9,64,2048]{2,1,0:T(8,128)}, f32[1024,1024]{1,0:T(8,128)}, /*index=5...) while((s32[]{:T(128)}, f32[1024,1024]{1,0:T(8,128)}, ...), condition=%wide.region_3.4_spmd.clone, body=%wide.region_2.3_spmd.clone.sunk | while | flops 584056832 | bytes 64225924 | solution.py:85
  578.8 8.2 %multiply_add_fusion.2 = (f32[1024,1024]{1,0:T(8,128)}, f32[1024,1024]{1,0:T(8,128)}) fusion(f32[1024,1024]{1,0:T(8,128)S(1)} %copy-done, f32[1024,1024]{1,0:T(8,128)} %get-tuple-element.210, f32[1024,1024]{1,0:T(8,128)} %get-tuple-element.199, f32[1024,1024]{1,0:T(8,128)} %get-tuple-element.198, pred[]{:T(512)S(6)} %compare.38), kind=kLoop, calls=%fused_computation.9.clone.1 | loop fusion | flops 8388608 | bytes 25165824 | tf_op jit(solution)/shard_map/while/body/eval_jaxpr/add | solution.py:81
  586.9 4.9 fusion.121
  595.4 10.6 %multiply_add_fusion.2 = (f32[1024,1024]{1,0:T(8,128)}, f32[1024,1024]{1,0:T(8,128)}) fusion(f32[1024,1024]{1,0:T(8,128)S(1)} %copy-done, f32[1024,1024]{1,0:T(8,128)} %get-tuple-element.210, f32[1024,1024]{1,0:T(8,128)} %get-tuple-element.199, f32[1024,1024]{1,0:T(8,128)} %get-tuple-element.198, pred[]{:T(512)S(6)} %compare.38), kind=kLoop, calls=%fused_computation.9.clone.1 | loop fusion | flops 8388608 | bytes 25165824 | tf_op jit(solution)/shard_map/while/body/eval_jaxpr/add | solution.py:81
  606.1 4.9 fusion.121
  614.5 10.6 %multiply_add_fusion.2 = (f32[1024,1024]{1,0:T(8,128)}, f32[1024,1024]{1,0:T(8,128)}) fusion(f32[1024,1024]{1,0:T(8,128)S(1)} %copy-done, f32[1024,1024]{1,0:T(8,128)} %get-tuple-element.210, f32[1024,1024]{1,0:T(8,128)} %get-tuple-element.199, f32[1024,1024]{1,0:T(8,128)} %get-tuple-element.198, pred[]{:T(512)S(6)} %compare.38), kind=kLoop, calls=%fused_computation.9.clone.1 | loop fusion | flops 8388608 | bytes 25165824 | tf_op jit(solution)/shard_map/while/body/eval_jaxpr/add | solution.py:81
  625.2 4.9 fusion.121
  633.7 10.6 %multiply_add_fusion.2 = (f32[1024,1024]{1,0:T(8,128)}, f32[1024,1024]{1,0:T(8,128)}) fusion(f32[1024,1024]{1,0:T(8,128)S(1)} %copy-done, f32[1024,1024]{1,0:T(8,128)} %get-tuple-element.210, f32[1024,1024]{1,0:T(8,128)} %get-tuple-element.199, f32[1024,1024]{1,0:T(8,128)} %get-tuple-element.198, pred[]{:T(512)S(6)} %compare.38), kind=kLoop, calls=%fused_computation.9.clone.1 | loop fusion | flops 8388608 | bytes 25165824 | tf_op jit(solution)/shard_map/while/body/eval_jaxpr/add | solution.py:81
  644.3 4.9 fusion.121
  652.8 10.6 %multiply_add_fusion.2 = (f32[1024,1024]{1,0:T(8,128)}, f32[1024,1024]{1,0:T(8,128)}) fusion(f32[1024,1024]{1,0:T(8,128)S(1)} %copy-done, f32[1024,1024]{1,0:T(8,128)} %get-tuple-element.210, f32[1024,1024]{1,0:T(8,128)} %get-tuple-element.199, f32[1024,1024]{1,0:T(8,128)} %get-tuple-element.198, pred[]{:T(512)S(6)} %compare.38), kind=kLoop, calls=%fused_computation.9.clone.1 | loop fusion | flops 8388608 | bytes 25165824 | tf_op jit(solution)/shard_map/while/body/eval_jaxpr/add | solution.py:81
  663.4 4.9 fusion.121
  671.9 10.6 %multiply_add_fusion.2 = (f32[1024,1024]{1,0:T(8,128)}, f32[1024,1024]{1,0:T(8,128)}) fusion(f32[1024,1024]{1,0:T(8,128)S(1)} %copy-done, f32[1024,1024]{1,0:T(8,128)} %get-tuple-element.210, f32[1024,1024]{1,0:T(8,128)} %get-tuple-element.199, f32[1024,1024]{1,0:T(8,128)} %get-tuple-element.198, pred[]{:T(512)S(6)} %compare.38), kind=kLoop, calls=%fused_computation.9.clone.1 | loop fusion | flops 8388608 | bytes 25165824 | tf_op jit(solution)/shard_map/while/body/eval_jaxpr/add | solution.py:81
  682.5 4.9 fusion.121
  691.0 10.6 %multiply_add_fusion.2 = (f32[1024,1024]{1,0:T(8,128)}, f32[1024,1024]{1,0:T(8,128)}) fusion(f32[1024,1024]{1,0:T(8,128)S(1)} %copy-done, f32[1024,1024]{1,0:T(8,128)} %get-tuple-element.210, f32[1024,1024]{1,0:T(8,128)} %get-tuple-element.199, f32[1024,1024]{1,0:T(8,128)} %get-tuple-element.198, pred[]{:T(512)S(6)} %compare.38), kind=kLoop, calls=%fused_computation.9.clone.1 | loop fusion | flops 8388608 | bytes 25165824 | tf_op jit(solution)/shard_map/while/body/eval_jaxpr/add | solution.py:81
  701.7 4.9 fusion.121
  710.2 10.6 %multiply_add_fusion.2 = (f32[1024,1024]{1,0:T(8,128)}, f32[1024,1024]{1,0:T(8,128)}) fusion(f32[1024,1024]{1,0:T(8,128)S(1)} %copy-done, f32[1024,1024]{1,0:T(8,128)} %get-tuple-element.210, f32[1024,1024]{1,0:T(8,128)} %get-tuple-element.199, f32[1024,1024]{1,0:T(8,128)} %get-tuple-element.198, pred[]{:T(512)S(6)} %compare.38), kind=kLoop, calls=%fused_computation.9.clone.1 | loop fusion | flops 8388608 | bytes 25165824 | tf_op jit(solution)/shard_map/while/body/eval_jaxpr/add | solution.py:81
  720.8 4.9 fusion.121
  729.3 10.6 %multiply_add_fusion.2 = (f32[1024,1024]{1,0:T(8,128)}, f32[1024,1024]{1,0:T(8,128)}) fusion(f32[1024,1024]{1,0:T(8,128)S(1)} %copy-done, f32[1024,1024]{1,0:T(8,128)} %get-tuple-element.210, f32[1024,1024]{1,0:T(8,128)} %get-tuple-element.199, f32[1024,1024]{1,0:T(8,128)} %get-tuple-element.198, pred[]{:T(512)S(6)} %compare.38), kind=kLoop, calls=%fused_computation.9.clone.1 | loop fusion | flops 8388608 | bytes 25165824 | tf_op jit(solution)/shard_map/while/body/eval_jaxpr/add | solution.py:81
  739.9 7.4 reshape.323
  747.3 13.0 %fusion.48 = f32[64,16,1024]{2,1,0:T(8,128)} fusion(f32[9,64,2,1024]{3,2,1,0:T(2,128)} %reshape.323, f32[16,1,9]{2,0,1:T(8,128)S(1)} %get-tuple-element.128, f32[16,1,9]{2,0,1:T(8,128)S(1)} %get-tuple-element.127), kind=kOutput, calls=%fused_computation.60 | convolution fusion | flops 226492704 | bytes 8914048 | tf_op jit(solution)/shard_map/tuk,kbud->btd/dot_general | solution.py:97
  (84 shorter events, 40.6 us)
Async XLA Ops:
  0.0 34.1 %copy-start.6 = (bf16[128,16,2048]{2,1,0:T(8,128)(2,1)S(1)}, bf16[128,16,2048]{2,1,0:T(8,128)(2,1)}, u32[]{:S(2)}) copy-start(bf16[128,16,2048]{2,1,0:T(8,128)(2,1)} %param.7) | copy-start | bytes 25165828
  98.4 7.1 copy-start.5
  98.4 189.3 %all-to-all-start = ((bf16[128,16,2,1024]{0,1,2,3:T(8,128)(2,1)}), bf16[128,16,2,1024]{0,1,2,3:T(8,128)(2,1)}, u32[]{:S(2)}, u32[]{:S(2)}) async-start(bf16[128,16,2,1024]{0,1,2,3:T(8,128)(2,1)} %copy.70), calls=%async_computation | async-start | bytes 16777216 | tf_op jit(solution)/shard_map/all_to_all | solution.py:112
  375.5 6.5 copy-start.3
  382.0 37.4 %copy-start.1 = (f32[2,4,16,64,256]{4,3,2,1,0:T(8,128)}, f32[2,4,16,64,256]{4,3,2,1,0:T(8,128)S(1)}, u32[]{:S(2)}) copy-start(f32[2,4,16,64,256]{4,3,2,1,0:T(8,128)S(1)} %get-tuple-element.121) | copy-start | bytes 25165828
  382.0 18.9 %copy-start.4 = (f32[4,4,1,1,1]{1,0,4,3,2:T(4,128)S(1)}, f32[4,4,1,1,1]{1,0,4,3,2:T(4,128)}, u32[]{:S(2)}) copy-start(f32[4,4,1,1,1]{1,0,4,3,2:T(4,128)} %constant.123) | copy-start | bytes 196
  470.7 5.4 copy-start.2
  504.2 58.2 %all-to-all-start.1 = ((bf16[16,2,36864]{2,1,0:T(2,128)(2,1)}), bf16[16,2,36864]{2,1,0:T(2,128)(2,1)S(1)}, u32[]{:S(2)}, u32[]{:S(2)}) async-start(bf16[16,2,36864]{2,1,0:T(2,128)(2,1)} %reshape.342), calls=%async_computation.1 | async-start | bytes 4718592 | tf_op jit(solution)/shard_map/all_to_all | solution.py:118
  576.3 2.4 copy-start
  593.0 2.5 copy-start
  612.1 2.4 copy-start
  631.2 2.4 copy-start
  650.3 2.4 copy-start
  669.4 2.4 copy-start
  688.5 2.5 copy-start
  707.7 2.5 copy-start
  726.8 2.5 copy-start
